TPU v7x, 256 devices: a whole 4x4x8 slice. The times are simulated.
256 devices in a mesh: row: 8 (over z), col: 32 (over x, y, core).
Axes of the slice: x: 4, y: 4, z: 8, core: 2. Of those that a mesh axis runs over, the one named last changes fastest.
Arguments:
- inputs: bfloat16 [1024, 16, 1024], P('col', 'row'), may hold values from -6 to 6
- weight: bfloat16 [1024, 27, 1024], P('col', None, 'row'), may hold values from -0.0390625 to 0.0390625
- grad_out: bfloat16 [1024, 16, 1024], P('col', 'row'), may hold values from -6 to 6
Outputs:
- outputs: bfloat16 [1024, 16, 1024], P('col', 'row')
- grad_in: bfloat16 [1024, 16, 1024], P('col', 'row')
- grad_weight: float32 [1024, 27, 1024], P('col', None, 'row')
All inputs are finite; a program needn't handle non-finite values.
Results may differ from a plain program's by a relative error of at most 0.0011.
Values may be sent and summed in bfloat16 or wider, within the bound.
A program may use at most 128 MiB of HBM per device.

v0:
```python
import math
import jax
import jax.numpy as jnp
from jax import lax
from jax.sharding import PartitionSpec as P

BX = 32
BY = 32
kernel_offsets = [(a, b, e) for a in (-1, 0, 1) for b in (-1, 0, 1) for e in (-1, 0, 1)]


def extended(block, sides, width):
    for axis, dim in sides:
        count = lax.axis_size(axis)
        forward = [(i, i + 1) for i in range(count - 1)]
        backward = [(target, source) for source, target in forward]
        low = lax.ppermute(
            lax.slice_in_dim(block, block.shape[dim] - width, None, axis=dim), axis, forward
        )
        high = lax.ppermute(lax.slice_in_dim(block, 0, width, axis=dim), axis, backward)
        block = jnp.concatenate([low, block, high], axis=dim)
    return block


def plane_valid(shift_y, shift_x, extent):
    positions = jnp.arange(extent, dtype=jnp.int32) % (BY * BX)
    along_y = positions // BX + shift_y
    along_x = positions % BX + shift_x
    return (along_y >= 0) & (along_y < BY) & (along_x >= 0) & (along_x < BX)


def flat_rim(field):
    flattened = field.reshape(field.shape[0], -1)
    return jnp.pad(flattened, ((0, 0), (BX + 1, BX + 1)))


def shifted(flattened, planes, shift_z, shift_y, shift_x):
    extent = planes * BY * BX
    offset = BX + 1 + (1 + shift_z) * BY * BX + shift_y * BX + shift_x
    window = lax.slice_in_dim(flattened, offset, offset + extent, axis=1)
    return jnp.where(plane_valid(shift_y, shift_x, extent)[None, :], window, jnp.zeros_like(window))


def forward_columns(padded, planes):
    windows = [shifted(padded, planes, sz, sy, sx) for sz, sy, sx in kernel_offsets]
    stacked = jnp.stack(windows, axis=0)
    return stacked.reshape(27 * padded.shape[0], stacked.shape[2])


def backward_columns(padded, planes):
    windows = [shifted(padded, planes, -sz, -sy, -sx) for sz, sy, sx in kernel_offsets]
    stacked = jnp.stack(windows, axis=1)
    return stacked.reshape(padded.shape[0] * 27, stacked.shape[2])


def group_count(shard_count, unit):
    target = max(1, 128 // unit)
    best = 1
    for candidate in range(1, shard_count + 1):
        if shard_count % candidate == 0 and candidate <= target:
            best = candidate
    return best


def on_device(inputs, weight, grad_out):
    width_dev = inputs.shape[0]
    planes = inputs.shape[1]
    extent = planes * BY * BX
    gathered_weight = lax.all_gather(weight, "row", axis=2, tiled=True)
    out_width = gathered_weight.shape[0]
    channels = gathered_weight.shape[2]
    input_rim = extended(inputs, (("row", 1),), 1)
    grad_rim = extended(grad_out, (("row", 1),), 1)
    grad_rows = grad_out.reshape(out_width, extent)
    initial = (
        jnp.zeros((out_width, extent), jnp.float32),
        jnp.zeros((channels, 27 * out_width), jnp.float32),
    )
    shard_rows = lax.all_gather(input_rim, "col", axis=0, tiled=True)
    shard_count = shard_rows.shape[0] // width_dev
    group = group_count(shard_count, width_dev)
    block_rows = group * width_dev
    count_blocks = shard_count // group

    def one_block(b, state):
        output_sum, weight_sum = state
        first_channel = b * block_rows
        channel_block = lax.dynamic_slice_in_dim(shard_rows, b * block_rows, block_rows, 0)
        columns = forward_columns(flat_rim(channel_block), planes)
        weight_block = lax.dynamic_slice_in_dim(gathered_weight, first_channel, block_rows, 2)
        flat_weight = weight_block.reshape(out_width, 27 * block_rows)
        output_sum = output_sum + jnp.dot(flat_weight, columns, preferred_element_type=jnp.float32)
        block_grad = lax.dot_general(
            columns, grad_rows, (((1,), (1,)), ((), ())), preferred_element_type=jnp.float32
        )
        block_grad = block_grad.reshape(27, block_rows, out_width).transpose(1, 0, 2)
        block_grad = block_grad.reshape(block_rows, 27 * out_width)
        weight_sum = lax.dynamic_update_slice_in_dim(weight_sum, block_grad, first_channel, 0)
        return (output_sum, weight_sum)

    output_sum, weight_rows_sum = lax.fori_loop(0, count_blocks, one_block, initial)
    outputs = output_sum.astype(jnp.bfloat16).reshape(out_width, planes, BY * BX)
    weight_sum = weight_rows_sum.reshape(channels, 27, out_width).transpose(2, 1, 0)
    scale = 1.0 / math.sqrt(planes * lax.axis_size("row") * BY * BX)
    grad_weight = lax.psum_scatter(weight_sum, "row", scatter_dimension=2, tiled=True) * scale
    grad_columns = backward_columns(flat_rim(grad_rim), planes)
    flat_cols = gathered_weight.reshape(out_width * 27, width_dev * lax.axis_size("col"))
    grad_sum = lax.psum_scatter(
        lax.dot_general(
            flat_cols, grad_columns, (((0,), (0,)), ((), ())), preferred_element_type=jnp.float32
        ),
        "col",
        scatter_dimension=0,
        tiled=True,
    )
    grad_in = grad_sum.astype(jnp.bfloat16).reshape(width_dev, planes, BY * BX)
    return (outputs, grad_in, grad_weight)


def solution(mesh):
    placed = (P("col", "row", None), P("col", None, "row"), P("col", "row", None))
    return jax.shard_map(
        on_device,
        mesh=mesh,
        in_specs=placed,
        out_specs=(P("col", "row", None), P("col", "row", None), P("col", None, "row")),
        check_vma=False,
    )
```

profile of v0, /device:TPU:1, one launch (start us, length us, event | category | flops | bytes accessed | tf_op | source)
XLA Modules:
  0.0 399.2 jit_solution(570935348018330792)
XLA Ops:
  10.5 5.0 %collective-permute-start = (bf16[32,1,1024]{2,1,0:T(2,128)(2,1)S(1)}, bf16[32,1,1024]{2,1,0:T(2,128)(2,1)S(1)}, u32[]{:S(2)}, u32[]{:S(2)}) collective-permute-start(bf16[32,1,1024]{2,1,0:T(2,128)(2,1)S(1)} %get-tuple-element.234), channel_id=1, source_target_pairs={{0,32},{32,64},{64,96},{96,128},{128,160},{160,192},{192,224},{1,3... | collective-permute-start | bytes 196616 | tf_op jit(solution)/shard_map/ppermute | solution.py:17
  22.1 4.4 %collective-permute-start.2 = (bf16[32,1,1024]{2,1,0:T(2,128)(2,1)S(1)}, bf16[32,1,1024]{2,1,0:T(2,128)(2,1)S(1)}, u32[]{:S(2)}, u32[]{:S(2)}) collective-permute-start(bf16[32,1,1024]{2,1,0:T(2,128)(2,1)S(1)} %get-tuple-element.232), channel_id=1, source_target_pairs={{0,32},{32,64},{64,96},{96,128},{128,160},{160,192},{192,224},{1,3... | collective-permute-start | bytes 196616 | tf_op jit(solution)/shard_map/ppermute | solution.py:17
  32.7 23.8 %all-gather.3.cloned.1.call-done = bf16[32,27,1024]{2,0,1:T(8,128)(2,1)} async-done(((bf16[32,27,128]{2,0,1:T(8,128)(2,1)}), bf16[32,27,1024]{2,0,1:T(8,128)(2,1)}) %all-gather.3.cloned.1.call-update) | async-done | bytes 1769488 | tf_op jit(solution)/shard_map/all_gather | solution.py:69
  56.5 8.2 %convolution_bitcast_fusion.1 = f32[1024,2048]{0,1:T(8,128)} fusion(bf16[32,27,2048]{2,0,1:T(8,128)(2,1)S(1)} %bitcast_dynamic-update-slice_fusion.8, bf16[32,27,1024]{2,0,1:T(8,128)(2,1)} %all-gather.3.cloned.1.call-done), kind=kOutput, calls=%fused_computation.105 | convolution fusion | flops 3623878656 | bytes 13697024 | tf_op jit(solution)/shard_map/dot_general | solution.py:109
  64.7 9.1 %copy.8 = f32[1024,2048]{1,0:T(8,128)} copy(f32[1024,2048]{0,1:T(8,128)} %convolution_bitcast_fusion.1) | data formatting | bytes 16777216
  73.9 46.7 %all-gather.5.cloned.1.call-done = bf16[1024,4,1024]{2,1,0:T(4,128)(2,1)} async-done(((bf16[32,4,1024]{2,1,0:T(4,128)(2,1)}), bf16[1024,4,1024]{2,1,0:T(4,128)(2,1)}) %all-gather.5.cloned.1.call-update) | async-done | bytes 8388624 | tf_op jit(solution)/shard_map/all_gather | solution.py:79
  121.0 219.4 %while.19 = (s32[]{:T(128)}, f32[32,2048]{1,0:T(8,128)}, f32[1024,864]{0,1:T(8,128)S(1)}, bf16[32,27,1024]{2,0,1:T(8,128)(2,1)}, bf16[1024,4,1024]{2,1,0:T(4,128...) while((s32[]{:T(128)}, f32[32,2048]{1,0:T(8,128)}, ...), condition=%wide.region_1.2_spmd.clone, body=%wide.region_0.1_spmd.clone.sunk | while | flops 913793024 | bytes 181059872 | solution.py:101
  129.5 5.0 %copy-done = bf16[27,128,2048]{2,1,0:T(8,128)(2,1)} copy-done((bf16[27,128,2048]{2,1,0:T(8,128)(2,1)}, bf16[27,128,2048]{2,1,0:T(8,128)(2,1)S(1)}, u32[]{:S(2)}) %copy-start) | copy-done | bytes 14155800 | tf_op jit(solution)/shard_map/while
  134.5 9.1 %fusion.147 = f32[32,2048]{1,0:T(8,128)} fusion(bf16[27,128,2048]{2,1,0:T(8,128)(2,1)} %copy-done, f32[32,2048]{1,0:T(8,128)} %get-tuple-element.284, bf16[32,27,1024]{2,0,1:T(8,128)(2,1)} %get-tuple-element.296, s32[]{:T(128)S(6)} %select_n.2038, pred[]{:T(512)S(6)} %compare.180), kind=kOutput, calls=%fused_computation.1.clone.1 | convolution fusion | flops 453115904 | bytes 14901253 | tf_op jit(solution)/shard_map/while/body/eval_jaxpr/dot_general | solution.py:92
  157.7 5.5 %copy-done = bf16[27,128,2048]{2,1,0:T(8,128)(2,1)} copy-done((bf16[27,128,2048]{2,1,0:T(8,128)(2,1)}, bf16[27,128,2048]{2,1,0:T(8,128)(2,1)S(1)}, u32[]{:S(2)}) %copy-start) | copy-done | bytes 14155800 | tf_op jit(solution)/shard_map/while
  163.2 8.8 %fusion.147 = f32[32,2048]{1,0:T(8,128)} fusion(bf16[27,128,2048]{2,1,0:T(8,128)(2,1)} %copy-done, f32[32,2048]{1,0:T(8,128)} %get-tuple-element.284, bf16[32,27,1024]{2,0,1:T(8,128)(2,1)} %get-tuple-element.296, s32[]{:T(128)S(6)} %select_n.2038, pred[]{:T(512)S(6)} %compare.180), kind=kOutput, calls=%fused_computation.1.clone.1 | convolution fusion | flops 453115904 | bytes 14901253 | tf_op jit(solution)/shard_map/while/body/eval_jaxpr/dot_general | solution.py:92
  185.6 5.1 %copy-done = bf16[27,128,2048]{2,1,0:T(8,128)(2,1)} copy-done((bf16[27,128,2048]{2,1,0:T(8,128)(2,1)}, bf16[27,128,2048]{2,1,0:T(8,128)(2,1)S(1)}, u32[]{:S(2)}) %copy-start) | copy-done | bytes 14155800 | tf_op jit(solution)/shard_map/while
  190.7 8.7 %fusion.147 = f32[32,2048]{1,0:T(8,128)} fusion(bf16[27,128,2048]{2,1,0:T(8,128)(2,1)} %copy-done, f32[32,2048]{1,0:T(8,128)} %get-tuple-element.284, bf16[32,27,1024]{2,0,1:T(8,128)(2,1)} %get-tuple-element.296, s32[]{:T(128)S(6)} %select_n.2038, pred[]{:T(512)S(6)} %compare.180), kind=kOutput, calls=%fused_computation.1.clone.1 | convolution fusion | flops 453115904 | bytes 14901253 | tf_op jit(solution)/shard_map/while/body/eval_jaxpr/dot_general | solution.py:92
  213.2 5.0 %copy-done = bf16[27,128,2048]{2,1,0:T(8,128)(2,1)} copy-done((bf16[27,128,2048]{2,1,0:T(8,128)(2,1)}, bf16[27,128,2048]{2,1,0:T(8,128)(2,1)S(1)}, u32[]{:S(2)}) %copy-start) | copy-done | bytes 14155800 | tf_op jit(solution)/shard_map/while
  218.2 8.7 %fusion.147 = f32[32,2048]{1,0:T(8,128)} fusion(bf16[27,128,2048]{2,1,0:T(8,128)(2,1)} %copy-done, f32[32,2048]{1,0:T(8,128)} %get-tuple-element.284, bf16[32,27,1024]{2,0,1:T(8,128)(2,1)} %get-tuple-element.296, s32[]{:T(128)S(6)} %select_n.2038, pred[]{:T(512)S(6)} %compare.180), kind=kOutput, calls=%fused_computation.1.clone.1 | convolution fusion | flops 453115904 | bytes 14901253 | tf_op jit(solution)/shard_map/while/body/eval_jaxpr/dot_general | solution.py:92
  240.4 5.0 %copy-done = bf16[27,128,2048]{2,1,0:T(8,128)(2,1)} copy-done((bf16[27,128,2048]{2,1,0:T(8,128)(2,1)}, bf16[27,128,2048]{2,1,0:T(8,128)(2,1)S(1)}, u32[]{:S(2)}) %copy-start) | copy-done | bytes 14155800 | tf_op jit(solution)/shard_map/while
  245.5 8.5 %fusion.147 = f32[32,2048]{1,0:T(8,128)} fusion(bf16[27,128,2048]{2,1,0:T(8,128)(2,1)} %copy-done, f32[32,2048]{1,0:T(8,128)} %get-tuple-element.284, bf16[32,27,1024]{2,0,1:T(8,128)(2,1)} %get-tuple-element.296, s32[]{:T(128)S(6)} %select_n.2038, pred[]{:T(512)S(6)} %compare.180), kind=kOutput, calls=%fused_computation.1.clone.1 | convolution fusion | flops 453115904 | bytes 14901253 | tf_op jit(solution)/shard_map/while/body/eval_jaxpr/dot_general | solution.py:92
  267.5 5.0 %copy-done = bf16[27,128,2048]{2,1,0:T(8,128)(2,1)} copy-done((bf16[27,128,2048]{2,1,0:T(8,128)(2,1)}, bf16[27,128,2048]{2,1,0:T(8,128)(2,1)S(1)}, u32[]{:S(2)}) %copy-start) | copy-done | bytes 14155800 | tf_op jit(solution)/shard_map/while
  272.5 8.5 %fusion.147 = f32[32,2048]{1,0:T(8,128)} fusion(bf16[27,128,2048]{2,1,0:T(8,128)(2,1)} %copy-done, f32[32,2048]{1,0:T(8,128)} %get-tuple-element.284, bf16[32,27,1024]{2,0,1:T(8,128)(2,1)} %get-tuple-element.296, s32[]{:T(128)S(6)} %select_n.2038, pred[]{:T(512)S(6)} %compare.180), kind=kOutput, calls=%fused_computation.1.clone.1 | convolution fusion | flops 453115904 | bytes 14901253 | tf_op jit(solution)/shard_map/while/body/eval_jaxpr/dot_general | solution.py:92
  294.5 5.0 %copy-done = bf16[27,128,2048]{2,1,0:T(8,128)(2,1)} copy-done((bf16[27,128,2048]{2,1,0:T(8,128)(2,1)}, bf16[27,128,2048]{2,1,0:T(8,128)(2,1)S(1)}, u32[]{:S(2)}) %copy-start) | copy-done | bytes 14155800 | tf_op jit(solution)/shard_map/while
  299.6 8.5 %fusion.147 = f32[32,2048]{1,0:T(8,128)} fusion(bf16[27,128,2048]{2,1,0:T(8,128)(2,1)} %copy-done, f32[32,2048]{1,0:T(8,128)} %get-tuple-element.284, bf16[32,27,1024]{2,0,1:T(8,128)(2,1)} %get-tuple-element.296, s32[]{:T(128)S(6)} %select_n.2038, pred[]{:T(512)S(6)} %compare.180), kind=kOutput, calls=%fused_computation.1.clone.1 | convolution fusion | flops 453115904 | bytes 14901253 | tf_op jit(solution)/shard_map/while/body/eval_jaxpr/dot_general | solution.py:92
  321.6 5.0 %copy-done = bf16[27,128,2048]{2,1,0:T(8,128)(2,1)} copy-done((bf16[27,128,2048]{2,1,0:T(8,128)(2,1)}, bf16[27,128,2048]{2,1,0:T(8,128)(2,1)S(1)}, u32[]{:S(2)}) %copy-start) | copy-done | bytes 14155800 | tf_op jit(solution)/shard_map/while
  326.6 8.5 %fusion.147 = f32[32,2048]{1,0:T(8,128)} fusion(bf16[27,128,2048]{2,1,0:T(8,128)(2,1)} %copy-done, f32[32,2048]{1,0:T(8,128)} %get-tuple-element.284, bf16[32,27,1024]{2,0,1:T(8,128)(2,1)} %get-tuple-element.296, s32[]{:T(128)S(6)} %select_n.2038, pred[]{:T(512)S(6)} %compare.180), kind=kOutput, calls=%fused_computation.1.clone.1 | convolution fusion | flops 453115904 | bytes 14901253 | tf_op jit(solution)/shard_map/while/body/eval_jaxpr/dot_general | solution.py:92
  346.0 44.9 %reduce-scatter.5.cloned.1.call-done = f32[32,27,128]{2,0,1:T(8,128)} async-done(((f32[32,27,1024]{2,0,1:T(8,128)}), f32[32,27,128]{2,0,1:T(8,128)}) %reduce-scatter.5.cloned.1.call-update) | async-done | bytes 442384 | tf_op jit(solution)/shard_map/reduce_scatter | solution.py:105
  (426 shorter events, 130.1 us)
Async XLA Ops:
  7.2 49.3 %all-gather.3.cloned.1.call-start = ((), (), s32[]{:S(2)}) async-start(), calls=%async_computation.2 | async-start | bytes 1990656 | tf_op jit(solution)/shard_map/all_gather | solution.py:69
  7.9 112.7 %all-gather.5.cloned.1.call-start = ((), (), s32[]{:S(2)}) async-start(), calls=%async_computation.3 | async-start | bytes 8650752 | tf_op jit(solution)/shard_map/all_gather | solution.py:79
  9.2 6.7 %collective-permute-start.1 = (bf16[32,1,1024]{2,1,0:T(2,128)(2,1)S(1)}, bf16[32,1,1024]{2,1,0:T(2,128)(2,1)S(1)}, u32[]{:S(2)}, u32[]{:S(2)}) collective-permute-start(bf16[32,1,1024]{2,1,0:T(2,128)(2,1)S(1)} %get-tuple-element.235), channel_id=1, source_target_pairs={{32,0},{64,32},{96,64},{128,96},{160,128},{192,160},{224,192},{33,... | collective-permute-start | bytes 196616 | tf_op jit(solution)/shard_map/ppermute | solution.py:20
  10.5 6.9 %collective-permute-start = (bf16[32,1,1024]{2,1,0:T(2,128)(2,1)S(1)}, bf16[32,1,1024]{2,1,0:T(2,128)(2,1)S(1)}, u32[]{:S(2)}, u32[]{:S(2)}) collective-permute-start(bf16[32,1,1024]{2,1,0:T(2,128)(2,1)S(1)} %get-tuple-element.234), channel_id=1, source_target_pairs={{0,32},{32,64},{64,96},{96,128},{128,160},{160,192},{192,224},{1,3... | collective-permute-start | bytes 196616 | tf_op jit(solution)/shard_map/ppermute | solution.py:17
  19.5 322.7 %reduce-scatter.7.cloned.1.call-start = ((), (), s32[]{:S(2)}) async-start(), calls=%async_computation.5 | async-start | bytes 8650752
  20.8 7.5 %collective-permute-start.3 = (bf16[32,1,1024]{2,1,0:T(2,128)(2,1)S(1)}, bf16[32,1,1024]{2,1,0:T(2,128)(2,1)S(1)}, u32[]{:S(2)}, u32[]{:S(2)}) collective-permute-start(bf16[32,1,1024]{2,1,0:T(2,128)(2,1)S(1)} %get-tuple-element.233), channel_id=1, source_target_pairs={{32,0},{64,32},{96,64},{128,96},{160,128},{192,160},{224,192},{33,... | collective-permute-start | bytes 196616 | tf_op jit(solution)/shard_map/ppermute | solution.py:20
  22.1 6.4 %collective-permute-start.2 = (bf16[32,1,1024]{2,1,0:T(2,128)(2,1)S(1)}, bf16[32,1,1024]{2,1,0:T(2,128)(2,1)S(1)}, u32[]{:S(2)}, u32[]{:S(2)}) collective-permute-start(bf16[32,1,1024]{2,1,0:T(2,128)(2,1)S(1)} %get-tuple-element.232), channel_id=1, source_target_pairs={{0,32},{32,64},{64,96},{96,128},{128,160},{160,192},{192,224},{1,3... | collective-permute-start | bytes 196616 | tf_op jit(solution)/shard_map/ppermute | solution.py:17
  73.8 317.0 %reduce-scatter.5.cloned.1.call-start = ((), (), s32[]{:S(2)}) async-start(), calls=%async_computation.4 | async-start | bytes 3981312 | tf_op jit(solution)/shard_map/reduce_scatter | solution.py:105
  134.5 10.5 %copy-start.1 = (bf16[27,128,2048]{2,1,0:T(8,128)(2,1)S(1)}, bf16[27,128,2048]{2,1,0:T(8,128)(2,1)}, u32[]{:S(2)}) copy-start(bf16[27,128,2048]{2,1,0:T(8,128)(2,1)} %copy-done) | copy-start | bytes 42467332 | tf_op jit(solution)/shard_map/while
  134.5 10.5 %copy-start.3 = (bf16[32,2048]{1,0:T(8,128)(2,1)S(1)}, bf16[32,2048]{1,0:T(8,128)(2,1)}, u32[]{:S(2)}) copy-start(bf16[32,2048]{1,0:T(8,128)(2,1)} %get-tuple-element.298) | copy-start | bytes 393220 | tf_op jit(solution)/shard_map/while
  163.2 9.6 %copy-start.1 = (bf16[27,128,2048]{2,1,0:T(8,128)(2,1)S(1)}, bf16[27,128,2048]{2,1,0:T(8,128)(2,1)}, u32[]{:S(2)}) copy-start(bf16[27,128,2048]{2,1,0:T(8,128)(2,1)} %copy-done) | copy-start | bytes 42467332 | tf_op jit(solution)/shard_map/while
  163.2 9.6 %copy-start.3 = (bf16[32,2048]{1,0:T(8,128)(2,1)S(1)}, bf16[32,2048]{1,0:T(8,128)(2,1)}, u32[]{:S(2)}) copy-start(bf16[32,2048]{1,0:T(8,128)(2,1)} %get-tuple-element.298) | copy-start | bytes 393220 | tf_op jit(solution)/shard_map/while
  190.6 9.8 %copy-start.1 = (bf16[27,128,2048]{2,1,0:T(8,128)(2,1)S(1)}, bf16[27,128,2048]{2,1,0:T(8,128)(2,1)}, u32[]{:S(2)}) copy-start(bf16[27,128,2048]{2,1,0:T(8,128)(2,1)} %copy-done) | copy-start | bytes 42467332 | tf_op jit(solution)/shard_map/while
  190.7 9.8 %copy-start.3 = (bf16[32,2048]{1,0:T(8,128)(2,1)S(1)}, bf16[32,2048]{1,0:T(8,128)(2,1)}, u32[]{:S(2)}) copy-start(bf16[32,2048]{1,0:T(8,128)(2,1)} %get-tuple-element.298) | copy-start | bytes 393220 | tf_op jit(solution)/shard_map/while
  218.2 9.5 %copy-start.1 = (bf16[27,128,2048]{2,1,0:T(8,128)(2,1)S(1)}, bf16[27,128,2048]{2,1,0:T(8,128)(2,1)}, u32[]{:S(2)}) copy-start(bf16[27,128,2048]{2,1,0:T(8,128)(2,1)} %copy-done) | copy-start | bytes 42467332 | tf_op jit(solution)/shard_map/while
  218.2 9.5 %copy-start.3 = (bf16[32,2048]{1,0:T(8,128)(2,1)S(1)}, bf16[32,2048]{1,0:T(8,128)(2,1)}, u32[]{:S(2)}) copy-start(bf16[32,2048]{1,0:T(8,128)(2,1)} %get-tuple-element.298) | copy-start | bytes 393220 | tf_op jit(solution)/shard_map/while
  245.5 9.3 %copy-start.1 = (bf16[27,128,2048]{2,1,0:T(8,128)(2,1)S(1)}, bf16[27,128,2048]{2,1,0:T(8,128)(2,1)}, u32[]{:S(2)}) copy-start(bf16[27,128,2048]{2,1,0:T(8,128)(2,1)} %copy-done) | copy-start | bytes 42467332 | tf_op jit(solution)/shard_map/while
  245.5 9.3 %copy-start.3 = (bf16[32,2048]{1,0:T(8,128)(2,1)S(1)}, bf16[32,2048]{1,0:T(8,128)(2,1)}, u32[]{:S(2)}) copy-start(bf16[32,2048]{1,0:T(8,128)(2,1)} %get-tuple-element.298) | copy-start | bytes 393220 | tf_op jit(solution)/shard_map/while
  272.5 9.3 %copy-start.1 = (bf16[27,128,2048]{2,1,0:T(8,128)(2,1)S(1)}, bf16[27,128,2048]{2,1,0:T(8,128)(2,1)}, u32[]{:S(2)}) copy-start(bf16[27,128,2048]{2,1,0:T(8,128)(2,1)} %copy-done) | copy-start | bytes 42467332 | tf_op jit(solution)/shard_map/while
  272.5 9.3 %copy-start.3 = (bf16[32,2048]{1,0:T(8,128)(2,1)S(1)}, bf16[32,2048]{1,0:T(8,128)(2,1)}, u32[]{:S(2)}) copy-start(bf16[32,2048]{1,0:T(8,128)(2,1)} %get-tuple-element.298) | copy-start | bytes 393220 | tf_op jit(solution)/shard_map/while
  299.6 9.3 %copy-start.1 = (bf16[27,128,2048]{2,1,0:T(8,128)(2,1)S(1)}, bf16[27,128,2048]{2,1,0:T(8,128)(2,1)}, u32[]{:S(2)}) copy-start(bf16[27,128,2048]{2,1,0:T(8,128)(2,1)} %copy-done) | copy-start | bytes 42467332 | tf_op jit(solution)/shard_map/while
  299.6 9.3 %copy-start.3 = (bf16[32,2048]{1,0:T(8,128)(2,1)S(1)}, bf16[32,2048]{1,0:T(8,128)(2,1)}, u32[]{:S(2)}) copy-start(bf16[32,2048]{1,0:T(8,128)(2,1)} %get-tuple-element.298) | copy-start | bytes 393220 | tf_op jit(solution)/shard_map/while
  326.6 9.3 %copy-start.1 = (bf16[27,128,2048]{2,1,0:T(8,128)(2,1)S(1)}, bf16[27,128,2048]{2,1,0:T(8,128)(2,1)}, u32[]{:S(2)}) copy-start(bf16[27,128,2048]{2,1,0:T(8,128)(2,1)} %copy-done) | copy-start | bytes 42467332 | tf_op jit(solution)/shard_map/while
  326.6 9.3 %copy-start.3 = (bf16[32,2048]{1,0:T(8,128)(2,1)S(1)}, bf16[32,2048]{1,0:T(8,128)(2,1)}, u32[]{:S(2)}) copy-start(bf16[32,2048]{1,0:T(8,128)(2,1)} %get-tuple-element.298) | copy-start | bytes 393220 | tf_op jit(solution)/shard_map/while
  (9 other events, 42.7 us)
Sparse Core Ops, SparseCore 0:
  9.7 46.7 all-gather.2
  59.0 61.5 all-gather.4
  124.6 97.8 reduce-scatter.6
  342.3 48.5 reduce-scatter.4
where the time goes:
time: 400 us; the launch traced here: 399 us
  waiting for transfers between devices  118 us (30%)
  matrix products  112 us (28%)
  local copies, waits for them, and re-layouts  82.8 us (21%)
  other arithmetic  57.2 us (14%)
  between operations  14.1 us (4%)
  starting transfers between devices  12.2 us (3%)
    dot_general x8, matrix products, one_block(): jnp.dot(flat_weight, columns, preferred_element_type=jnp.float32)  69.5 us
    while x56, local copies, waits for them, and re-layouts  51.2 us
    all_gather x1, waiting for transfers between devices, on_device(): shard_rows = lax.all_gather(input_rim, 'col', axis=0, tiled=True)  46.7 us
    while x208, other arithmetic  45.3 us
    reduce_scatter x1, waiting for transfers between devices, on_device(): lax.psum_scatter(weight_sum, 'row', scatter_dimension=2, tiled=True) * scale  44.9 us
    dot_general x8, matrix products, one_block(): lax.dot_general(columns, grad_rows, (((1,), (1,)), ((), ())), preferred_e...  34.4 us
    all_gather x1, waiting for transfers between devices, on_device(): gathered_weight = lax.all_gather(weight, 'row', axis=2, tiled=True)  23.8 us
    unnamed x7, local copies, waits for them, and re-layouts  14.6 us
  transfers between devices with their start and end apart: 8, of which 6 were waited for; matrix products, arithmetic and copies ran while one was open for 50% of the time, Pallas kernels for 0%

commit v1 on v0

--- a/solution.py
+++ b/solution.py
@@ -66,7 +66,12 @@
     width_dev = inputs.shape[0]
     planes = inputs.shape[1]
     extent = planes * BY * BX
-    gathered_weight = lax.all_gather(weight, "row", axis=2, tiled=True)
+    ring = [weight]
+    for hop in range(7):
+        ring.append(lax.ppermute(ring[-1], "row", [(dev, (dev + 1) % 8) for dev in range(8)]))
+    gathered_weight = jnp.roll(
+        jnp.concatenate(ring[::-1], axis=2), (lax.axis_index("row") + 1) * ring[0].shape[2], axis=2
+    )
     out_width = gathered_weight.shape[0]
     channels = gathered_weight.shape[2]
     input_rim = extended(inputs, (("row", 1),), 1)

time: 400 us -> 375 us (0.938)
  waiting for transfers between devices: 118 us -> 94 us
  local copies, waits for them, and re-layouts: 82.8 us -> 74.7 us
  starting transfers between devices: 12.2 us -> 19.4 us
    all_gather x1, waiting for transfers between devices: 46.7 us -> 6.7 us  [on_device(): shard_rows = lax.all_gather(input_rim, 'col', axis=0, tiled=True)]
    ppermute x0 -> x7, waiting for transfers between devices: none -> 37.2 us  [on_device(): lax.ppermute(ring[-1], 'row', [(dev, (dev + 1) % 8) for dev in range(8)])]
    all_gather x1 -> x0, waiting for transfers between devices: 23.8 us -> none  [on_device(): gathered_weight = lax.all_gather(weight, 'row', axis=2, tiled=True)]
    unnamed x7 -> x23, local copies, waits for them, and re-layouts: 14.6 us -> 5.7 us
    ppermute x0 -> x7, starting transfers between devices: none -> 8.36 us  [on_device(): lax.ppermute(ring[-1], 'row', [(dev, (dev + 1) % 8) for dev in range(8)])]
    reduce_scatter x1, waiting for transfers between devices: 44.9 us -> 50.1 us  [on_device(): lax.psum_scatter(weight_sum, 'row', scatter_dimension=2, tiled=True) * scale]
  transfers between devices with their start and end apart: 8 -> 14, of which waited for: 6 -> 8; matrix products, arithmetic and copies ran while one was open for 50% -> 51% of each run, Pallas kernels for 0% -> 0%
where the time goes in v1:
time: 375 us; the launch traced here: 374 us
  matrix products  111 us (30%)
  waiting for transfers between devices  94 us (25%)
  local copies, waits for them, and re-layouts  74.7 us (20%)
  other arithmetic  58.2 us (16%)
  starting transfers between devices  19.4 us (5%)
  between operations  14.3 us (4%)
    dot_general x8, matrix products, one_block(): jnp.dot(flat_weight, columns, preferred_element_type=jnp.float32)  69.7 us
    while x56, local copies, waits for them, and re-layouts  51.1 us
    reduce_scatter x1, waiting for transfers between devices, on_device(): lax.psum_scatter(weight_sum, 'row', scatter_dimension=2, tiled=True) * scale  50.1 us
    while x208, other arithmetic  45.3 us
    ppermute x7, waiting for transfers between devices, on_device(): lax.ppermute(ring[-1], 'row', [(dev, (dev + 1) % 8) for dev in range(8)])  37.2 us
    dot_general x8, matrix products, one_block(): lax.dot_general(columns, grad_rows, (((1,), (1,)), ((), ())), preferred_e...  34.4 us
    dynamic_slice x8, local copies, waits for them, and re-layouts, one_block(): lax.dynamic_slice_in_dim(shard_rows, b * block_rows, block_rows, 0)  12.8 us
    ppermute x7, starting transfers between devices, on_device(): lax.ppermute(ring[-1], 'row', [(dev, (dev + 1) % 8) for dev in range(8)])  8.36 us
  transfers between devices with their start and end apart: 14, of which 8 were waited for; matrix products, arithmetic and copies ran while one was open for 51% of the time, Pallas kernels for 0%

profile of v1, /device:TPU:1, one launch (start us, length us, event | category | flops | bytes accessed | tf_op | source)
XLA Modules:
  0.0 374.0 jit_solution(11690811873182958182)
XLA Ops:
  44.9 5.7 %collective-permute-done.3 = bf16[32,27,128]{2,0,1:T(8,128)(2,1)S(1)} collective-permute-done((bf16[32,27,128]{2,0,1:T(8,128)(2,1)S(1)}, bf16[32,27,128]{2,0,1:T(8,128)(2,1)S(1)}, u32[]{:S(2)}, u32[]{:S(2)}) %collective-permute-start.3) | collective-permute-done | bytes 221216 | tf_op jit(solution)/shard_map/ppermute | solution.py:71
  50.7 7.6 %collective-permute-done.4 = bf16[32,27,128]{2,0,1:T(8,128)(2,1)S(1)} collective-permute-done((bf16[32,27,128]{2,0,1:T(8,128)(2,1)S(1)}, bf16[32,27,128]{2,0,1:T(8,128)(2,1)S(1)}, u32[]{:S(2)}, u32[]{:S(2)}) %collective-permute-start.4) | collective-permute-done | bytes 221216 | tf_op jit(solution)/shard_map/ppermute | solution.py:71
  58.5 8.0 %collective-permute-done.5 = bf16[32,27,128]{2,0,1:T(8,128)(2,1)S(1)} collective-permute-done((bf16[32,27,128]{2,0,1:T(8,128)(2,1)S(1)}, bf16[32,27,128]{2,0,1:T(8,128)(2,1)S(1)}, u32[]{:S(2)}, u32[]{:S(2)}) %collective-permute-start.5) | collective-permute-done | bytes 221216 | tf_op jit(solution)/shard_map/ppermute | solution.py:71
  66.5 7.8 %collective-permute-done.6 = bf16[32,27,128]{2,0,1:T(8,128)(2,1)S(1)} collective-permute-done((bf16[32,27,128]{2,0,1:T(8,128)(2,1)S(1)}, bf16[32,27,128]{2,0,1:T(8,128)(2,1)S(1)}, u32[]{:S(2)}, u32[]{:S(2)}) %collective-permute-start.6) | collective-permute-done | bytes 221216 | tf_op jit(solution)/shard_map/ppermute | solution.py:71
  77.1 6.8 %convolution_bitcast_fusion.1 = f32[1024,2048]{1,0:T(8,128)} fusion(bf16[32,27,1024]{2,0,1:T(8,128)(2,1)S(1)} %constant_dynamic-slice_fusion.1, bf16[32,27,2048]{2,0,1:T(8,128)(2,1)S(1)} %bitcast_dynamic-update-slice_fusion.8), kind=kOutput, calls=%fused_computation.105 | convolution fusion | flops 3623878656 | bytes 13697024 | tf_op jit(solution)/shard_map/dot_general | solution.py:114
  83.9 6.7 %all-gather.2.cloned.1.call-done = bf16[1024,4,1024]{2,1,0:T(4,128)(2,1)} async-done(((bf16[32,4,1024]{2,1,0:T(4,128)(2,1)}), bf16[1024,4,1024]{2,1,0:T(4,128)(2,1)}) %all-gather.2.cloned.1.call-update) | async-done | bytes 8388624 | tf_op jit(solution)/shard_map/all_gather | solution.py:84
  91.0 219.3 %while.19 = (s32[]{:T(128)}, f32[32,2048]{1,0:T(8,128)}, f32[1024,864]{0,1:T(8,128)S(1)}, bf16[32,27,1024]{2,0,1:T(8,128)(2,1)}, bf16[1024,4,1024]{2,1,0:T(4,128...) while((s32[]{:T(128)}, f32[32,2048]{1,0:T(8,128)}, ...), condition=%wide.region_1.2_spmd.clone, body=%wide.region_0.1_spmd.clone.sunk | while | flops 913793024 | bytes 181059872 | solution.py:106
  99.3 5.0 %copy-done = bf16[27,128,2048]{2,1,0:T(8,128)(2,1)} copy-done((bf16[27,128,2048]{2,1,0:T(8,128)(2,1)}, bf16[27,128,2048]{2,1,0:T(8,128)(2,1)S(1)}, u32[]{:S(2)}) %copy-start) | copy-done | bytes 14155800 | tf_op jit(solution)/shard_map/while
  104.4 9.0 %fusion.147 = f32[32,2048]{1,0:T(8,128)} fusion(bf16[27,128,2048]{2,1,0:T(8,128)(2,1)} %copy-done, f32[32,2048]{1,0:T(8,128)} %get-tuple-element.278, bf16[32,27,1024]{2,0,1:T(8,128)(2,1)} %get-tuple-element.290, s32[]{:T(128)S(6)} %select_n.2052, pred[]{:T(512)S(6)} %compare.181), kind=kOutput, calls=%fused_computation.1.clone.1 | convolution fusion | flops 453115904 | bytes 14901253 | tf_op jit(solution)/shard_map/while/body/eval_jaxpr/dot_general | solution.py:97
  127.5 5.5 %copy-done = bf16[27,128,2048]{2,1,0:T(8,128)(2,1)} copy-done((bf16[27,128,2048]{2,1,0:T(8,128)(2,1)}, bf16[27,128,2048]{2,1,0:T(8,128)(2,1)S(1)}, u32[]{:S(2)}) %copy-start) | copy-done | bytes 14155800 | tf_op jit(solution)/shard_map/while
  133.0 9.1 %fusion.147 = f32[32,2048]{1,0:T(8,128)} fusion(bf16[27,128,2048]{2,1,0:T(8,128)(2,1)} %copy-done, f32[32,2048]{1,0:T(8,128)} %get-tuple-element.278, bf16[32,27,1024]{2,0,1:T(8,128)(2,1)} %get-tuple-element.290, s32[]{:T(128)S(6)} %select_n.2052, pred[]{:T(512)S(6)} %compare.181), kind=kOutput, calls=%fused_computation.1.clone.1 | convolution fusion | flops 453115904 | bytes 14901253 | tf_op jit(solution)/shard_map/while/body/eval_jaxpr/dot_general | solution.py:97
  155.6 5.0 %copy-done = bf16[27,128,2048]{2,1,0:T(8,128)(2,1)} copy-done((bf16[27,128,2048]{2,1,0:T(8,128)(2,1)}, bf16[27,128,2048]{2,1,0:T(8,128)(2,1)S(1)}, u32[]{:S(2)}) %copy-start) | copy-done | bytes 14155800 | tf_op jit(solution)/shard_map/while
  160.6 8.8 %fusion.147 = f32[32,2048]{1,0:T(8,128)} fusion(bf16[27,128,2048]{2,1,0:T(8,128)(2,1)} %copy-done, f32[32,2048]{1,0:T(8,128)} %get-tuple-element.278, bf16[32,27,1024]{2,0,1:T(8,128)(2,1)} %get-tuple-element.290, s32[]{:T(128)S(6)} %select_n.2052, pred[]{:T(512)S(6)} %compare.181), kind=kOutput, calls=%fused_computation.1.clone.1 | convolution fusion | flops 453115904 | bytes 14901253 | tf_op jit(solution)/shard_map/while/body/eval_jaxpr/dot_general | solution.py:97
  183.2 5.0 %copy-done = bf16[27,128,2048]{2,1,0:T(8,128)(2,1)} copy-done((bf16[27,128,2048]{2,1,0:T(8,128)(2,1)}, bf16[27,128,2048]{2,1,0:T(8,128)(2,1)S(1)}, u32[]{:S(2)}) %copy-start) | copy-done | bytes 14155800 | tf_op jit(solution)/shard_map/while
  188.2 8.7 %fusion.147 = f32[32,2048]{1,0:T(8,128)} fusion(bf16[27,128,2048]{2,1,0:T(8,128)(2,1)} %copy-done, f32[32,2048]{1,0:T(8,128)} %get-tuple-element.278, bf16[32,27,1024]{2,0,1:T(8,128)(2,1)} %get-tuple-element.290, s32[]{:T(128)S(6)} %select_n.2052, pred[]{:T(512)S(6)} %compare.181), kind=kOutput, calls=%fused_computation.1.clone.1 | convolution fusion | flops 453115904 | bytes 14901253 | tf_op jit(solution)/shard_map/while/body/eval_jaxpr/dot_general | solution.py:97
  210.4 5.0 %copy-done = bf16[27,128,2048]{2,1,0:T(8,128)(2,1)} copy-done((bf16[27,128,2048]{2,1,0:T(8,128)(2,1)}, bf16[27,128,2048]{2,1,0:T(8,128)(2,1)S(1)}, u32[]{:S(2)}) %copy-start) | copy-done | bytes 14155800 | tf_op jit(solution)/shard_map/while
  215.5 8.5 %fusion.147 = f32[32,2048]{1,0:T(8,128)} fusion(bf16[27,128,2048]{2,1,0:T(8,128)(2,1)} %copy-done, f32[32,2048]{1,0:T(8,128)} %get-tuple-element.278, bf16[32,27,1024]{2,0,1:T(8,128)(2,1)} %get-tuple-element.290, s32[]{:T(128)S(6)} %select_n.2052, pred[]{:T(512)S(6)} %compare.181), kind=kOutput, calls=%fused_computation.1.clone.1 | convolution fusion | flops 453115904 | bytes 14901253 | tf_op jit(solution)/shard_map/while/body/eval_jaxpr/dot_general | solution.py:97
  237.5 5.0 %copy-done = bf16[27,128,2048]{2,1,0:T(8,128)(2,1)} copy-done((bf16[27,128,2048]{2,1,0:T(8,128)(2,1)}, bf16[27,128,2048]{2,1,0:T(8,128)(2,1)S(1)}, u32[]{:S(2)}) %copy-start) | copy-done | bytes 14155800 | tf_op jit(solution)/shard_map/while
  242.5 8.5 %fusion.147 = f32[32,2048]{1,0:T(8,128)} fusion(bf16[27,128,2048]{2,1,0:T(8,128)(2,1)} %copy-done, f32[32,2048]{1,0:T(8,128)} %get-tuple-element.278, bf16[32,27,1024]{2,0,1:T(8,128)(2,1)} %get-tuple-element.290, s32[]{:T(128)S(6)} %select_n.2052, pred[]{:T(512)S(6)} %compare.181), kind=kOutput, calls=%fused_computation.1.clone.1 | convolution fusion | flops 453115904 | bytes 14901253 | tf_op jit(solution)/shard_map/while/body/eval_jaxpr/dot_general | solution.py:97
  264.5 5.0 %copy-done = bf16[27,128,2048]{2,1,0:T(8,128)(2,1)} copy-done((bf16[27,128,2048]{2,1,0:T(8,128)(2,1)}, bf16[27,128,2048]{2,1,0:T(8,128)(2,1)S(1)}, u32[]{:S(2)}) %copy-start) | copy-done | bytes 14155800 | tf_op jit(solution)/shard_map/while
  269.6 8.5 %fusion.147 = f32[32,2048]{1,0:T(8,128)} fusion(bf16[27,128,2048]{2,1,0:T(8,128)(2,1)} %copy-done, f32[32,2048]{1,0:T(8,128)} %get-tuple-element.278, bf16[32,27,1024]{2,0,1:T(8,128)(2,1)} %get-tuple-element.290, s32[]{:T(128)S(6)} %select_n.2052, pred[]{:T(512)S(6)} %compare.181), kind=kOutput, calls=%fused_computation.1.clone.1 | convolution fusion | flops 453115904 | bytes 14901253 | tf_op jit(solution)/shard_map/while/body/eval_jaxpr/dot_general | solution.py:97
  291.6 5.0 %copy-done = bf16[27,128,2048]{2,1,0:T(8,128)(2,1)} copy-done((bf16[27,128,2048]{2,1,0:T(8,128)(2,1)}, bf16[27,128,2048]{2,1,0:T(8,128)(2,1)S(1)}, u32[]{:S(2)}) %copy-start) | copy-done | bytes 14155800 | tf_op jit(solution)/shard_map/while
  296.6 8.5 %fusion.147 = f32[32,2048]{1,0:T(8,128)} fusion(bf16[27,128,2048]{2,1,0:T(8,128)(2,1)} %copy-done, f32[32,2048]{1,0:T(8,128)} %get-tuple-element.278, bf16[32,27,1024]{2,0,1:T(8,128)(2,1)} %get-tuple-element.290, s32[]{:T(128)S(6)} %select_n.2052, pred[]{:T(512)S(6)} %compare.181), kind=kOutput, calls=%fused_computation.1.clone.1 | convolution fusion | flops 453115904 | bytes 14901253 | tf_op jit(solution)/shard_map/while/body/eval_jaxpr/dot_general | solution.py:97
  315.5 50.1 %reduce-scatter.5.cloned.1.call-done = f32[32,27,128]{2,0,1:T(8,128)} async-done(((f32[32,27,1024]{2,0,1:T(8,128)}), f32[32,27,128]{2,0,1:T(8,128)}) %reduce-scatter.5.cloned.1.call-update) | async-done | bytes 442384 | tf_op jit(solution)/shard_map/reduce_scatter | solution.py:110
  (457 shorter events, 154.1 us)
Async XLA Ops:
  7.2 83.4 %all-gather.2.cloned.1.call-start = ((), (), s32[]{:S(2)}) async-start(), calls=%async_computation.2 | async-start | bytes 8650752 | tf_op jit(solution)/shard_map/all_gather | solution.py:84
  7.2 23.6 %collective-permute-start = (bf16[32,27,128]{2,0,1:T(8,128)(2,1)}, bf16[32,27,128]{2,0,1:T(8,128)(2,1)S(1)}, u32[]{:S(2)}, u32[]{:S(2)}) collective-permute-start(bf16[32,27,128]{2,0,1:T(8,128)(2,1)} %param.6), channel_id=1, source_target_pairs={{0,32},{32,64},{64,96},{96,128},{128,160},{160,192},{192,224},{224... | collective-permute-start | bytes 663560 | tf_op jit(solution)/shard_map/ppermute | solution.py:71
  11.0 14.0 %collective-permute-start.8 = (bf16[32,1,1024]{2,1,0:T(2,128)(2,1)S(1)}, bf16[32,1,1024]{2,1,0:T(2,128)(2,1)S(1)}, u32[]{:S(2)}, u32[]{:S(2)}) collective-permute-start(bf16[32,1,1024]{2,1,0:T(2,128)(2,1)S(1)} %get-tuple-element.229), channel_id=1, source_target_pairs={{32,0},{64,32},{96,64},{128,96},{160,128},{192,160},{224,192},{33,... | collective-permute-start | bytes 196616 | tf_op jit(solution)/shard_map/ppermute | solution.py:20
  12.3 12.7 %collective-permute-start.7 = (bf16[32,1,1024]{2,1,0:T(2,128)(2,1)S(1)}, bf16[32,1,1024]{2,1,0:T(2,128)(2,1)S(1)}, u32[]{:S(2)}, u32[]{:S(2)}) collective-permute-start(bf16[32,1,1024]{2,1,0:T(2,128)(2,1)S(1)} %get-tuple-element.228), channel_id=1, source_target_pairs={{0,32},{32,64},{64,96},{96,128},{128,160},{160,192},{192,224},{1,3... | collective-permute-start | bytes 196616 | tf_op jit(solution)/shard_map/ppermute | solution.py:17
  17.7 9.4 %collective-permute-start.10 = (bf16[32,1,1024]{2,1,0:T(2,128)(2,1)S(1)}, bf16[32,1,1024]{2,1,0:T(2,128)(2,1)S(1)}, u32[]{:S(2)}, u32[]{:S(2)}) collective-permute-start(bf16[32,1,1024]{2,1,0:T(2,128)(2,1)S(1)} %get-tuple-element.227), channel_id=1, source_target_pairs={{32,0},{64,32},{96,64},{128,96},{160,128},{192,160},{224,192},{33,... | collective-permute-start | bytes 196616 | tf_op jit(solution)/shard_map/ppermute | solution.py:20
  19.0 8.1 %collective-permute-start.9 = (bf16[32,1,1024]{2,1,0:T(2,128)(2,1)S(1)}, bf16[32,1,1024]{2,1,0:T(2,128)(2,1)S(1)}, u32[]{:S(2)}, u32[]{:S(2)}) collective-permute-start(bf16[32,1,1024]{2,1,0:T(2,128)(2,1)S(1)} %get-tuple-element.226), channel_id=1, source_target_pairs={{0,32},{32,64},{64,96},{96,128},{128,160},{160,192},{192,224},{1,3... | collective-permute-start | bytes 196616 | tf_op jit(solution)/shard_map/ppermute | solution.py:17
  27.0 285.1 %reduce-scatter.3.cloned.1.call-start = ((), (), s32[]{:S(2)}) async-start(), calls=%async_computation.3 | async-start | bytes 8650752 | tf_op jit(solution)/shard_map/reduce_scatter | solution.py:113
  30.0 44.9 %copy-start.5 = (bf16[32,27,128]{2,0,1:T(8,128)(2,1)S(1)}, bf16[32,27,128]{2,0,1:T(8,128)(2,1)}, u32[]{:S(2)}) copy-start(bf16[32,27,128]{2,0,1:T(8,128)(2,1)} %param.6) | copy-start | bytes 663556
  30.8 6.8 %collective-permute-start.1 = (bf16[32,27,128]{2,0,1:T(8,128)(2,1)S(1)}, bf16[32,27,128]{2,0,1:T(8,128)(2,1)S(1)}, u32[]{:S(2)}, u32[]{:S(2)}) collective-permute-start(bf16[32,27,128]{2,0,1:T(8,128)(2,1)S(1)} %collective-permute-done), channel_id=1, source_target_pairs={{0,32},{32,64},{64,96},{96,128},{128,160},{160,192},{192,224},{224... | collective-permute-start | bytes 663560 | tf_op jit(solution)/shard_map/ppermute | solution.py:71
  37.6 6.0 %collective-permute-start.2 = (bf16[32,27,128]{2,0,1:T(8,128)(2,1)S(1)}, bf16[32,27,128]{2,0,1:T(8,128)(2,1)S(1)}, u32[]{:S(2)}, u32[]{:S(2)}) collective-permute-start(bf16[32,27,128]{2,0,1:T(8,128)(2,1)S(1)} %collective-permute-done.1), channel_id=1, source_target_pairs={{0,32},{32,64},{64,96},{96,128},{128,160},{160,192},{192,224},{224... | collective-permute-start | bytes 663560 | tf_op jit(solution)/shard_map/ppermute | solution.py:71
  43.6 7.0 %collective-permute-start.3 = (bf16[32,27,128]{2,0,1:T(8,128)(2,1)S(1)}, bf16[32,27,128]{2,0,1:T(8,128)(2,1)S(1)}, u32[]{:S(2)}, u32[]{:S(2)}) collective-permute-start(bf16[32,27,128]{2,0,1:T(8,128)(2,1)S(1)} %collective-permute-done.2), channel_id=1, source_target_pairs={{0,32},{32,64},{64,96},{96,128},{128,160},{160,192},{192,224},{224... | collective-permute-start | bytes 663560 | tf_op jit(solution)/shard_map/ppermute | solution.py:71
  50.6 7.7 %collective-permute-start.4 = (bf16[32,27,128]{2,0,1:T(8,128)(2,1)S(1)}, bf16[32,27,128]{2,0,1:T(8,128)(2,1)S(1)}, u32[]{:S(2)}, u32[]{:S(2)}) collective-permute-start(bf16[32,27,128]{2,0,1:T(8,128)(2,1)S(1)} %collective-permute-done.3), channel_id=1, source_target_pairs={{0,32},{32,64},{64,96},{96,128},{128,160},{160,192},{192,224},{224... | collective-permute-start | bytes 663560 | tf_op jit(solution)/shard_map/ppermute | solution.py:71
  58.3 8.1 %collective-permute-start.5 = (bf16[32,27,128]{2,0,1:T(8,128)(2,1)S(1)}, bf16[32,27,128]{2,0,1:T(8,128)(2,1)S(1)}, u32[]{:S(2)}, u32[]{:S(2)}) collective-permute-start(bf16[32,27,128]{2,0,1:T(8,128)(2,1)S(1)} %collective-permute-done.4), channel_id=1, source_target_pairs={{0,32},{32,64},{64,96},{96,128},{128,160},{160,192},{192,224},{224... | collective-permute-start | bytes 663560 | tf_op jit(solution)/shard_map/ppermute | solution.py:71
  66.4 7.9 %collective-permute-start.6 = (bf16[32,27,128]{2,0,1:T(8,128)(2,1)S(1)}, bf16[32,27,128]{2,0,1:T(8,128)(2,1)S(1)}, u32[]{:S(2)}, u32[]{:S(2)}) collective-permute-start(bf16[32,27,128]{2,0,1:T(8,128)(2,1)S(1)} %collective-permute-done.5), channel_id=1, source_target_pairs={{0,32},{32,64},{64,96},{96,128},{128,160},{160,192},{192,224},{224... | collective-permute-start | bytes 663560 | tf_op jit(solution)/shard_map/ppermute | solution.py:71
  83.9 281.8 %reduce-scatter.5.cloned.1.call-start = ((), (), s32[]{:S(2)}) async-start(), calls=%async_computation.4 | async-start | bytes 3981312 | tf_op jit(solution)/shard_map/reduce_scatter | solution.py:110
  104.4 10.4 %copy-start.1 = (bf16[27,128,2048]{2,1,0:T(8,128)(2,1)S(1)}, bf16[27,128,2048]{2,1,0:T(8,128)(2,1)}, u32[]{:S(2)}) copy-start(bf16[27,128,2048]{2,1,0:T(8,128)(2,1)} %copy-done) | copy-start | bytes 42467332 | tf_op jit(solution)/shard_map/while
  104.4 10.4 %copy-start.3 = (bf16[32,2048]{1,0:T(8,128)(2,1)S(1)}, bf16[32,2048]{1,0:T(8,128)(2,1)}, u32[]{:S(2)}) copy-start(bf16[32,2048]{1,0:T(8,128)(2,1)} %get-tuple-element.292) | copy-start | bytes 393220 | tf_op jit(solution)/shard_map/while
  133.0 9.9 %copy-start.1 = (bf16[27,128,2048]{2,1,0:T(8,128)(2,1)S(1)}, bf16[27,128,2048]{2,1,0:T(8,128)(2,1)}, u32[]{:S(2)}) copy-start(bf16[27,128,2048]{2,1,0:T(8,128)(2,1)} %copy-done) | copy-start | bytes 42467332 | tf_op jit(solution)/shard_map/while
  133.0 9.9 %copy-start.3 = (bf16[32,2048]{1,0:T(8,128)(2,1)S(1)}, bf16[32,2048]{1,0:T(8,128)(2,1)}, u32[]{:S(2)}) copy-start(bf16[32,2048]{1,0:T(8,128)(2,1)} %get-tuple-element.292) | copy-start | bytes 393220 | tf_op jit(solution)/shard_map/while
  160.6 9.9 %copy-start.1 = (bf16[27,128,2048]{2,1,0:T(8,128)(2,1)S(1)}, bf16[27,128,2048]{2,1,0:T(8,128)(2,1)}, u32[]{:S(2)}) copy-start(bf16[27,128,2048]{2,1,0:T(8,128)(2,1)} %copy-done) | copy-start | bytes 42467332 | tf_op jit(solution)/shard_map/while
  160.6 9.9 %copy-start.3 = (bf16[32,2048]{1,0:T(8,128)(2,1)S(1)}, bf16[32,2048]{1,0:T(8,128)(2,1)}, u32[]{:S(2)}) copy-start(bf16[32,2048]{1,0:T(8,128)(2,1)} %get-tuple-element.292) | copy-start | bytes 393220 | tf_op jit(solution)/shard_map/while
  188.2 9.5 %copy-start.1 = (bf16[27,128,2048]{2,1,0:T(8,128)(2,1)S(1)}, bf16[27,128,2048]{2,1,0:T(8,128)(2,1)}, u32[]{:S(2)}) copy-start(bf16[27,128,2048]{2,1,0:T(8,128)(2,1)} %copy-done) | copy-start | bytes 42467332 | tf_op jit(solution)/shard_map/while
  188.2 9.5 %copy-start.3 = (bf16[32,2048]{1,0:T(8,128)(2,1)S(1)}, bf16[32,2048]{1,0:T(8,128)(2,1)}, u32[]{:S(2)}) copy-start(bf16[32,2048]{1,0:T(8,128)(2,1)} %get-tuple-element.292) | copy-start | bytes 393220 | tf_op jit(solution)/shard_map/while
  215.5 9.3 %copy-start.3 = (bf16[32,2048]{1,0:T(8,128)(2,1)S(1)}, bf16[32,2048]{1,0:T(8,128)(2,1)}, u32[]{:S(2)}) copy-start(bf16[32,2048]{1,0:T(8,128)(2,1)} %get-tuple-element.292) | copy-start | bytes 393220 | tf_op jit(solution)/shard_map/while
  (17 other events, 109.1 us)
Sparse Core Ops, SparseCore 0:
  27.2 63.3 all-gather.1
  94.6 99.2 reduce-scatter.2
  312.2 53.3 reduce-scatter.4
